TPU v7x, 32 devices: a whole 2x2x4 slice. The times are simulated.
32 devices in a mesh: tp: 4 (over y, core), fsdp: 8 (over z, x).
Axes of the slice: x: 2, y: 2, z: 4, core: 2. Of those that a mesh axis runs over, the one named last changes fastest.
Arguments:
- momentum: float32 [8192, 28672], P('tp', 'fsdp'), may hold values from -6 to 6
- gradient: bfloat16 [8192, 28672], P('tp', 'fsdp'), may hold values from -6 to 6
- basis: float32 [28672, 512], P('fsdp', 'tp'), may hold values from -1 to 1
Outputs:
- new_momentum: float32 [8192, 28672], P('tp', 'fsdp')
- new_basis: float32 [28672, 512], P('fsdp', 'tp')
- left_factor: float32 [8192, 512], P(('tp', 'fsdp'))
All inputs are finite; a program needn't handle non-finite values.
Results may differ from a plain program's by a relative error of at most 0.0003.
Values sent between devices are 32-bit elements; how exact they have to be, the bound alone decides.
A program may use at most 192 MiB of HBM per device.

v0:
```python
import jax
import jax.numpy as jnp
from jax import lax
from jax.sharding import PartitionSpec as P

keep_rate = 0.95
tiny = 1e-06
high = lax.Precision.HIGHEST


def solve_right(left, gram):
    lower = jnp.linalg.cholesky(gram)
    return jax.scipy.linalg.solve_triangular(lower, left.T, lower=True).T


def local_gram(left):
    return jnp.dot(left.T, left, precision=high, preferred_element_type=jnp.float32)


def gram_over_rows(left):
    return lax.psum(local_gram(left), "tp")


def on_device(momentum, gradient, basis):
    tile = momentum + gradient.astype(jnp.float32)
    partial_value = jnp.dot(
        tile,
        lax.all_gather(basis, "tp", axis=1, tiled=True),
        precision=high,
        preferred_element_type=jnp.float32,
    )
    share_rows = tile.shape[0] // lax.axis_size("fsdp")
    whole = lax.psum(partial_value, "fsdp")
    for turn in range(2):
        whole = solve_right(whole, gram_over_rows(whole))
    own_left = lax.dynamic_slice_in_dim(whole, lax.axis_index("fsdp") * share_rows, share_rows, 0)
    partial_right = jnp.dot(tile.T, whole, precision=high, preferred_element_type=jnp.float32)
    mine = lax.psum_scatter(partial_right, "tp", scatter_dimension=1, tiled=True)
    squares = lax.psum(jnp.sum(mine * mine, axis=0), "fsdp")
    new_basis = mine / jnp.sqrt(squares + tiny)[None, :]
    full_right = lax.all_gather(mine, "tp", axis=1, tiled=True)
    new_momentum = tile - (1.0 - keep_rate) * jnp.dot(
        whole, full_right.T, precision=high, preferred_element_type=jnp.float32
    )
    return (new_momentum, new_basis, own_left)


def solution(mesh):
    placed = (P("tp", "fsdp"), P("tp", "fsdp"), P("fsdp", "tp"))
    return jax.shard_map(
        on_device,
        mesh=mesh,
        in_specs=placed,
        out_specs=(P("tp", "fsdp"), P("fsdp", "tp"), P(("tp", "fsdp"), None)),
        check_vma=False,
    )
```

profile of v0, /device:TPU:0, one launch (start us, length us, event | category | flops | bytes accessed | tf_op | source)
XLA Modules:
  0.0 1009.8 jit_solution(1744838277263823175)
XLA Ops:
  7.9 57.6 %all-gather.3.cloned.1.call-done = f32[3584,512]{1,0:T(8,128)} async-done(((f32[3584,128]{1,0:T(8,128)}), f32[3584,512]{1,0:T(8,128)}) %all-gather.3.cloned.1.call-update) | async-done | bytes 7340048 | tf_op jit(solution)/shard_map/all_gather | solution.py:28
  65.6 53.8 %fusion.1 = f32[2048,512]{1,0:T(8,128)} fusion(f32[3584,512]{1,0:T(8,128)} %all-gather.3.cloned.1.call-done, f32[2048,3584]{1,0:T(8,128)} %param.6, bf16[2048,3584]{1,0:T(8,128)(2,1)} %param.7), kind=kOutput, calls=%fused_computation.7 | convolution fusion | flops 45111836672 | bytes 55574528 | tf_op jit(solution)/shard_map/dot_general | solution.py:26
  119.4 156.5 %all-reduce.5.cloned.1.call-done = f32[2048,512]{1,0:T(8,128)} async-done(((f32[2048,512]{1,0:T(8,128)}), f32[2048,512]{1,0:T(8,128)}) %all-reduce.5.cloned.1.call-update) | async-done | bytes 4194320 | tf_op jit(solution)/shard_map/psum | solution.py:33
  275.9 11.4 %fusion.88 = f32[512,512]{0,1:T(8,128)} fusion(f32[2048,512]{1,0:T(8,128)} %all-reduce.5.cloned.1.call-done), kind=kOutput, calls=%fused_computation.151 | convolution fusion | flops 6442450944 | bytes 5242880 | tf_op jit(solution)/shard_map/dot_general | solution.py:17
  287.8 34.9 %all-reduce.7.cloned.1.call-done = f32[512,512]{0,1:T(8,128)} async-done(((f32[512,512]{0,1:T(8,128)}), f32[512,512]{0,1:T(8,128)}) %all-reduce.7.cloned.1.call-update) | async-done | bytes 1048592 | tf_op jit(solution)/shard_map/psum | solution.py:21
  325.8 11.7 %cholesky.286 = f32[128,128]{1,0:T(8,128)S(1)} custom-call(f32[128,128]{1,0:T(8,128)S(1)} %cholesky.426), custom_call_target="Cholesky" | custom-call | tf_op jit(solution)/shard_map/jit(cholesky)/cholesky | solution.py:12
  348.2 11.7 %cholesky.305 = f32[128,128]{1,0:T(8,128)S(1)} custom-call(f32[128,128]{1,0:T(8,128)S(1)} %cholesky.430), custom_call_target="Cholesky" | custom-call | tf_op jit(solution)/shard_map/jit(cholesky)/cholesky | solution.py:12
  359.9 10.0 custom-call.28
  370.5 11.7 %cholesky.326 = f32[128,128]{1,0:T(8,128)S(1)} custom-call(f32[128,128]{1,0:T(8,128)S(1)} %cholesky.435), custom_call_target="Cholesky" | custom-call | tf_op jit(solution)/shard_map/jit(cholesky)/cholesky | solution.py:12
  392.7 11.7 %cholesky.343 = f32[128,128]{1,0:T(8,128)S(1)} custom-call(f32[128,128]{1,0:T(8,128)S(1)} %convolution_subtract_fusion.9), custom_call_target="Cholesky" | custom-call | tf_op jit(solution)/shard_map/jit(cholesky)/cholesky | solution.py:12
  417.3 39.3 %custom-call.30 = f32[4,128,128]{1,2,0:T(8,128)S(1)} custom-call(f32[4,128,128]{2,1,0:T(8,128)S(1)} %get-tuple-element.19), custom_call_target="InvertDiagBlocksLowerTriangular" | custom-call | tf_op jit(solution)/shard_map/jit(_solve_triangular)/triangular_solve | solution.py:13
  483.7 36.7 %all-reduce.9.cloned.1.call-done = f32[512,512]{0,1:T(8,128)} async-done(((f32[512,512]{0,1:T(8,128)}), f32[512,512]{0,1:T(8,128)}) %all-reduce.9.cloned.1.call-update) | async-done | bytes 1048592 | tf_op jit(solution)/shard_map/psum | solution.py:21
  524.4 11.7 %cholesky.358 = f32[128,128]{1,0:T(8,128)S(1)} custom-call(f32[128,128]{1,0:T(8,128)S(1)} %cholesky.439), custom_call_target="Cholesky" | custom-call | tf_op jit(solution)/shard_map/jit(cholesky)/cholesky | solution.py:12
  548.6 11.7 %cholesky.377 = f32[128,128]{1,0:T(8,128)S(1)} custom-call(f32[128,128]{1,0:T(8,128)S(1)} %cholesky.443), custom_call_target="Cholesky" | custom-call | tf_op jit(solution)/shard_map/jit(cholesky)/cholesky | solution.py:12
  560.4 10.0 custom-call.32
  572.0 11.7 %cholesky.398 = f32[128,128]{1,0:T(8,128)S(1)} custom-call(f32[128,128]{1,0:T(8,128)S(1)} %cholesky.448), custom_call_target="Cholesky" | custom-call | tf_op jit(solution)/shard_map/jit(cholesky)/cholesky | solution.py:12
  595.0 11.7 %cholesky.415 = f32[128,128]{1,0:T(8,128)S(1)} custom-call(f32[128,128]{1,0:T(8,128)S(1)} %convolution_subtract_fusion.8), custom_call_target="Cholesky" | custom-call | tf_op jit(solution)/shard_map/jit(cholesky)/cholesky | solution.py:12
  613.5 11.7 %while.5 = (s32[]{:T(128)}, f32[512,512]{1,0:T(8,128)}, s32[4,2]{0,1:T(2,128)S(1)}, f32[4,128,128]{2,1,0:T(8,128)S(1)}, s32[]{:T(128)}) while((s32[]{:T(128)}, f32[512,512]{1,0:T(8,128)}, s32[4,2]{0,1:T(2,128)S(1)}, f32[4,128,128]{2,1,0:T(8,128)S(1)}, s32[]{:T(128)}) %tuple.74), condition=%wide.while_cond.clone, body=%wide.while_body.clone.sunk | while | flops 2 | bytes 131189 | solution.py:13
  625.2 39.3 %custom-call.34 = f32[4,128,128]{1,2,0:T(8,128)S(1)} custom-call(f32[4,128,128]{2,1,0:T(8,128)S(1)} %get-tuple-element.20), custom_call_target="InvertDiagBlocksLowerTriangular" | custom-call | tf_op jit(solution)/shard_map/jit(_solve_triangular)/triangular_solve | solution.py:13
  677.2 107.3 %fusion = f32[3584,512]{1,0:T(8,128)} fusion(f32[2048,3584]{1,0:T(8,128)} %param.6, bf16[2048,3584]{1,0:T(8,128)(2,1)} %param.7, f32[128,2048]{1,0:T(8,128)S(1)} %fusion.54, f32[128,2048]{1,0:T(8,128)S(1)} %fusion.55, f32[128,2048]{1,0:T(8,128)S(1)} %fusion.57, f32[128,2048]{1,0:T(8,128)S(1)} %fusion.58), kind=kOutput, calls=%fused_computation.6 | convolution fusion | flops 45114982400 | bytes 55574528 | tf_op jit(solution)/shard_map/dot_general | solution.py:37
  784.6 65.2 %reduce-scatter.2.cloned.1.call-done = f32[3584,128]{1,0:T(8,128)} async-done(((f32[3584,512]{1,0:T(8,128)}), f32[3584,128]{1,0:T(8,128)}) %reduce-scatter.2.cloned.1.call-update) | async-done | bytes 1835024 | tf_op jit(solution)/shard_map/reduce_scatter | solution.py:38
  856.2 21.4 %psum.31 = f32[128]{0:T(128)S(1)} all-reduce(f32[128]{0:T(128)S(1)} %multiply_reduce_fusion), channel_id=1, replica_groups=mesh['tp'=4,'fsdp'=8] {'fsdp'}, use_global_device_ids=true, to_apply=%region_13.16 | all-reduce | flops 128 | bytes 1024 | tf_op jit(solution)/shard_map/psum | solution.py:39
  880.4 24.1 %all-gather.5.cloned.1.call-done = f32[3584,512]{1,0:T(8,128)} async-done(((f32[3584,128]{1,0:T(8,128)}), f32[3584,512]{1,0:T(8,128)}) %all-gather.5.cloned.1.call-update) | async-done | bytes 7340048 | tf_op jit(solution)/shard_map/all_gather | solution.py:41
  904.5 98.3 %multiply_subtract_fusion = f32[2048,3584]{1,0:T(8,128)} fusion(f32[3584,512]{1,0:T(8,128)} %all-gather.5.cloned.1.call-done, f32[2048,3584]{1,0:T(8,128)} %param.6, bf16[2048,3584]{1,0:T(8,128)(2,1)} %param.7, f32[128,2048]{1,0:T(8,128)} %copy-done.2, f32[128,2048]{1,0:T(8,128)S(1)} %fusion.55, f32[128,2048]{1,0:T(8,128)S(1)} %fusion.57, ...), kind=kOutput, calls=%fused_computation.4 | convolution fusion | flops 45129662464 | bytes 84934656 | tf_op jit(solution)/shard_map/dot_general | solution.py:42
  (119 shorter events, 138.2 us)
Async XLA Ops:
  7.2 58.4 %all-gather.3.cloned.1.call-start = ((), (), s32[]{:S(2)}) async-start(), calls=%async_computation.1 | async-start | bytes 9175040 | tf_op jit(solution)/shard_map/all_gather | solution.py:28
  7.9 268.0 %all-reduce.5.cloned.1.call-start = ((), (), s32[]{:S(2)}) async-start(), calls=%async_computation.2 | async-start | bytes 8388608 | tf_op jit(solution)/shard_map/psum | solution.py:33
  119.4 203.4 %all-reduce.7.cloned.1.call-start = ((), (), s32[]{:S(2)}) async-start(), calls=%async_computation.3 | async-start | bytes 2097152 | tf_op jit(solution)/shard_map/psum | solution.py:21
  287.3 233.1 %all-reduce.9.cloned.1.call-start = ((), (), s32[]{:S(2)}) async-start(), calls=%async_computation.4 | async-start | bytes 2097152 | tf_op jit(solution)/shard_map/psum | solution.py:21
  456.7 6.6 copy-start
  467.9 6.9 copy-start.1
  474.7 1.0 copy-start.3
  483.5 366.2 %reduce-scatter.2.cloned.1.call-start = ((), (), s32[]{:S(2)}) async-start(), calls=%async_computation.5 | async-start | bytes 9175040 | tf_op jit(solution)/shard_map/reduce_scatter | solution.py:38
  523.4 1.0 copy-start.5
  667.5 4.7 copy-start.4
  676.2 1.0 copy-start.2
  784.5 119.9 %all-gather.5.cloned.1.call-start = ((), (), s32[]{:S(2)}) async-start(), calls=%async_computation.6 | async-start | bytes 9175040 | tf_op jit(solution)/shard_map/all_gather | solution.py:41
Sparse Core Ops, SparseCore 0:
  9.5 56.0 all-gather.2
  119.5 156.3 all-reduce.4
  287.4 35.2 all-reduce.6
  483.6 36.7 all-reduce.8
  784.6 65.0 reduce-scatter.1
  851.1 53.2 all-gather.4
where the time goes:
time: 1020 us; the launch traced here: 1010 us
  waiting for transfers between devices  376 us (37%)
  matrix products  315 us (31%)
  other arithmetic  247 us (24%)
  local copies, waits for them, and re-layouts  28.8 us (3%)
  blocking collectives  21.4 us (2%)
  between operations  20 us (2%)
    another operation x29, other arithmetic, solve_right(): lower = jnp.linalg.cholesky(gram)  158 us
    psum x1, waiting for transfers between devices, on_device(): whole = lax.psum(partial_value, 'fsdp')  156 us
    dot_general x1, matrix products, on_device(): jnp.dot(tile.T, whole, precision=high, preferred_element_type=jnp.float32)  107 us
    dot_general x1, matrix products, on_device(): jnp.dot(whole, full_right.T, precision=high, preferred_element_type=jnp.f...  98.3 us
    another operation x6, other arithmetic, solve_right(): return jax.scipy.linalg.solve_triangular(lower, left.T, lower=True).T  81.9 us
    psum x2, waiting for transfers between devices, gram_over_rows(): return lax.psum(local_gram(left), 'tp')  71.6 us
    reduce_scatter x1, waiting for transfers between devices, on_device(): lax.psum_scatter(partial_right, 'tp', scatter_dimension=1, tiled=True)  65.2 us
    all_gather x1, waiting for transfers between devices, on_device(): lax.all_gather(basis, 'tp', axis=1, tiled=True)  57.6 us
  transfers between devices with their start and end apart: 6, of which 6 were waited for; matrix products, arithmetic and copies ran while one was open for 1% of the time, Pallas kernels for 0%

commit v1 on v0

--- a/solution.py
+++ b/solution.py
@@ -2,10 +2,20 @@
 import jax.numpy as jnp
 from jax import lax
 from jax.sharding import PartitionSpec as P
+from jax.lax import axis_size, ppermute
 
 keep_rate = 0.95
 tiny = 1e-06
 high = lax.Precision.HIGHEST
+
+
+def move_the_point(x_part, which_axis):
+    degree = axis_size(which_axis)
+    even = x_part
+    for p in [at for at in (1, 2, 4, 8, 16) if at < degree]:
+        val = ppermute(even, which_axis, list(map(lambda no: (no, no ^ p), range(degree))))
+        even = even + val
+    return even
 
 
 def solve_right(left, gram):
@@ -30,7 +40,7 @@
         preferred_element_type=jnp.float32,
     )
     share_rows = tile.shape[0] // lax.axis_size("fsdp")
-    whole = lax.psum(partial_value, "fsdp")
+    whole = move_the_point(partial_value, "fsdp")
     for turn in range(2):
         whole = solve_right(whole, gram_over_rows(whole))
     own_left = lax.dynamic_slice_in_dim(whole, lax.axis_index("fsdp") * share_rows, share_rows, 0)

time: 1020 us -> 1250 us (1.23)
  waiting for transfers between devices: 376 us -> 576 us
  matrix products: 315 us -> 330 us
    ppermute x0 -> x3, waiting for transfers between devices: none -> 361 us  [move_the_point(): ppermute(even, which_axis, list(map(lambda no: (no, no ^ p), range(degree...]
    psum x1 -> x0, waiting for transfers between devices: 156 us -> none  [on_device(): whole = lax.psum(partial_value, 'fsdp')]
    dot_general x2, matrix products: 19.2 us -> 32.6 us  [local_gram(): jnp.dot(left.T, left, precision=high, preferred_element_type=jnp.float32)]
  transfers between devices with their start and end apart: 6 -> 8, of which waited for: 6 -> 8; matrix products, arithmetic and copies ran while one was open for 1% -> 1% of each run, Pallas kernels for 0% -> 0%
where the time goes in v1:
time: 1250 us; the launch traced here: 1240 us
  waiting for transfers between devices  576 us (46%)
  matrix products  330 us (26%)
  other arithmetic  258 us (21%)
  local copies, waits for them, and re-layouts  29.3 us (2%)
  blocking collectives  21.4 us (2%)
  between operations  19.5 us (2%)
    ppermute x3, waiting for transfers between devices, move_the_point(): ppermute(even, which_axis, list(map(lambda no: (no, no ^ p), range(degree...  361 us
    another operation x29, other arithmetic, solve_right(): lower = jnp.linalg.cholesky(gram)  158 us
    dot_general x1, matrix products, on_device(): jnp.dot(tile.T, whole, precision=high, preferred_element_type=jnp.float32)  107 us
    dot_general x1, matrix products, on_device(): jnp.dot(whole, full_right.T, precision=high, preferred_element_type=jnp.f...  98.3 us
    another operation x6, other arithmetic, solve_right(): return jax.scipy.linalg.solve_triangular(lower, left.T, lower=True).T  81.9 us
    psum x2, waiting for transfers between devices, gram_over_rows(): return lax.psum(local_gram(left), 'tp')  66.6 us
    reduce_scatter x1, waiting for transfers between devices, on_device(): lax.psum_scatter(partial_right, 'tp', scatter_dimension=1, tiled=True)  65.2 us
    all_gather x1, waiting for transfers between devices, on_device(): lax.all_gather(basis, 'tp', axis=1, tiled=True)  57.6 us
  transfers between devices with their start and end apart: 8, of which 8 were waited for; matrix products, arithmetic and copies ran while one was open for 1% of the time, Pallas kernels for 0%

profile of v1, /device:TPU:0, one launch (start us, length us, event | category | flops | bytes accessed | tf_op | source)
XLA Modules:
  0.0 1240.1 jit_solution(7234896255357869918)
XLA Ops:
  7.9 57.6 %all-gather.3.cloned.1.call-done = f32[3584,512]{1,0:T(8,128)} async-done(((f32[3584,128]{1,0:T(8,128)}), f32[3584,512]{1,0:T(8,128)}) %all-gather.3.cloned.1.call-update) | async-done | bytes 7340048 | tf_op jit(solution)/shard_map/all_gather | solution.py:38
  65.6 56.1 %fusion.1 = f32[2048,512]{1,0:T(8,128)S(1)} fusion(f32[3584,512]{1,0:T(8,128)} %all-gather.3.cloned.1.call-done, f32[2048,3584]{1,0:T(8,128)} %param.6, bf16[2048,3584]{1,0:T(8,128)(2,1)} %param.7), kind=kOutput, calls=%fused_computation.7 | convolution fusion | flops 45111836672 | bytes 55574528 | tf_op jit(solution)/shard_map/dot_general | solution.py:36
  123.2 91.3 %collective-permute-done = f32[2048,512]{1,0:T(8,128)S(1)} collective-permute-done((f32[2048,512]{1,0:T(8,128)S(1)}, f32[2048,512]{1,0:T(8,128)S(1)}, u32[]{:S(2)}, u32[]{:S(2)}) %collective-permute-start) | collective-permute-done | bytes 4194336 | tf_op jit(solution)/shard_map/ppermute | solution.py:16
  217.1 90.4 %collective-permute-done.1 = f32[2048,512]{1,0:T(8,128)S(1)} collective-permute-done((f32[2048,512]{1,0:T(8,128)S(1)}, f32[2048,512]{1,0:T(8,128)S(1)}, u32[]{:S(2)}, u32[]{:S(2)}) %collective-permute-start.1) | collective-permute-done | bytes 4194336 | tf_op jit(solution)/shard_map/ppermute | solution.py:16
  312.9 179.7 %collective-permute-done.2 = f32[2048,512]{1,0:T(8,128)} collective-permute-done((f32[2048,512]{1,0:T(8,128)}, f32[2048,512]{1,0:T(8,128)}, u32[]{:S(2)}, u32[]{:S(2)}) %collective-permute-start.2) | collective-permute-done | bytes 4194336 | tf_op jit(solution)/shard_map/ppermute | solution.py:16
  492.6 24.8 %fusion.32 = f32[512,512]{0,1:T(8,128)} fusion(f32[2048,512]{1,0:T(8,128)} %add.63, f32[2048,512]{1,0:T(8,128)} %collective-permute-done.2), kind=kOutput, calls=%fused_computation.40 | convolution fusion | flops 6443499520 | bytes 9437184 | tf_op jit(solution)/shard_map/dot_general | solution.py:27
  523.9 29.9 %all-reduce.4.cloned.1.call-done = f32[512,512]{0,1:T(8,128)} async-done(((f32[512,512]{0,1:T(8,128)}), f32[512,512]{0,1:T(8,128)}) %all-reduce.4.cloned.1.call-update) | async-done | bytes 1048592 | tf_op jit(solution)/shard_map/psum | solution.py:31
  556.8 11.7 cholesky.286
  579.2 11.7 cholesky.305
  601.8 11.7 cholesky.326
  624.0 11.9 cholesky.343
  649.1 39.3 %custom-call.30 = f32[4,128,128]{1,2,0:T(8,128)S(1)} custom-call(f32[4,128,128]{2,1,0:T(8,128)S(1)} %get-tuple-element.19), custom_call_target="InvertDiagBlocksLowerTriangular" | custom-call | tf_op jit(solution)/shard_map/jit(_solve_triangular)/triangular_solve | solution.py:23
  714.4 36.7 %all-reduce.6.cloned.1.call-done = f32[512,512]{0,1:T(8,128)} async-done(((f32[512,512]{0,1:T(8,128)}), f32[512,512]{0,1:T(8,128)}) %all-reduce.6.cloned.1.call-update) | async-done | bytes 1048592 | tf_op jit(solution)/shard_map/psum | solution.py:31
  755.1 11.7 cholesky.358
  779.3 11.7 cholesky.377
  802.6 11.7 cholesky.398
  825.6 11.7 cholesky.415
  844.2 11.7 while.5
  855.9 39.3 %custom-call.34 = f32[4,128,128]{1,2,0:T(8,128)S(1)} custom-call(f32[4,128,128]{2,1,0:T(8,128)S(1)} %get-tuple-element.20), custom_call_target="InvertDiagBlocksLowerTriangular" | custom-call | tf_op jit(solution)/shard_map/jit(_solve_triangular)/triangular_solve | solution.py:23
  907.8 107.3 %fusion = f32[3584,512]{1,0:T(8,128)} fusion(f32[2048,3584]{1,0:T(8,128)} %param.6, bf16[2048,3584]{1,0:T(8,128)(2,1)} %param.7, f32[128,2048]{1,0:T(8,128)S(1)} %fusion.57, f32[128,2048]{1,0:T(8,128)S(1)} %fusion.58, f32[128,2048]{1,0:T(8,128)S(1)} %fusion.60, f32[128,2048]{1,0:T(8,128)S(1)} %fusion.61), kind=kOutput, calls=%fused_computation.6 | convolution fusion | flops 45114982400 | bytes 55574528 | tf_op jit(solution)/shard_map/dot_general | solution.py:47
  1015.2 65.2 %reduce-scatter.2.cloned.1.call-done = f32[3584,128]{1,0:T(8,128)} async-done(((f32[3584,512]{1,0:T(8,128)}), f32[3584,128]{1,0:T(8,128)}) %reduce-scatter.2.cloned.1.call-update) | async-done | bytes 1835024 | tf_op jit(solution)/shard_map/reduce_scatter | solution.py:48
  1086.8 21.4 %psum.23 = f32[128]{0:T(128)S(1)} all-reduce(f32[128]{0:T(128)S(1)} %multiply_reduce_fusion), channel_id=1, replica_groups=mesh['tp'=4,'fsdp'=8] {'fsdp'}, use_global_device_ids=true, to_apply=%region_12.15 | all-reduce | flops 128 | bytes 1024 | tf_op jit(solution)/shard_map/psum | solution.py:49
  1111.0 24.1 %all-gather.5.cloned.1.call-done = f32[3584,512]{1,0:T(8,128)} async-done(((f32[3584,128]{1,0:T(8,128)}), f32[3584,512]{1,0:T(8,128)}) %all-gather.5.cloned.1.call-update) | async-done | bytes 7340048 | tf_op jit(solution)/shard_map/all_gather | solution.py:51
  1135.1 98.3 %multiply_subtract_fusion = f32[2048,3584]{1,0:T(8,128)} fusion(f32[3584,512]{1,0:T(8,128)} %all-gather.5.cloned.1.call-done, f32[2048,3584]{1,0:T(8,128)} %param.6, bf16[2048,3584]{1,0:T(8,128)(2,1)} %param.7, f32[128,2048]{1,0:T(8,128)} %copy-done.2, f32[128,2048]{1,0:T(8,128)S(1)} %fusion.58, f32[128,2048]{1,0:T(8,128)S(1)} %fusion.60, ...), kind=kOutput, calls=%fused_computation.4 | convolution fusion | flops 45129662464 | bytes 84934656 | tf_op jit(solution)/shard_map/dot_general | solution.py:52
  (125 shorter events, 173.8 us)
Async XLA Ops:
  7.2 58.4 %all-gather.3.cloned.1.call-start = ((), (), s32[]{:S(2)}) async-start(), calls=%async_computation.1 | async-start | bytes 9175040 | tf_op jit(solution)/shard_map/all_gather | solution.py:38
  7.9 545.9 %all-reduce.4.cloned.1.call-start = ((), (), s32[]{:S(2)}) async-start(), calls=%async_computation.2 | async-start | bytes 2097152 | tf_op jit(solution)/shard_map/psum | solution.py:31
  121.7 92.8 %collective-permute-start = (f32[2048,512]{1,0:T(8,128)S(1)}, f32[2048,512]{1,0:T(8,128)S(1)}, u32[]{:S(2)}, u32[]{:S(2)}) collective-permute-start(f32[2048,512]{1,0:T(8,128)S(1)} %fusion.1), channel_id=1, source_target_pairs={{0,1},{1,0},{2,3},{3,2},{4,5},{5,4},{6,7},{7,6},{8,9},{9,8},{10,11... | collective-permute-start | bytes 12582920 | tf_op jit(solution)/shard_map/ppermute | solution.py:16
  215.5 91.9 %collective-permute-start.1 = (f32[2048,512]{1,0:T(8,128)S(1)}, f32[2048,512]{1,0:T(8,128)S(1)}, u32[]{:S(2)}, u32[]{:S(2)}) collective-permute-start(f32[2048,512]{1,0:T(8,128)S(1)} %add.62), channel_id=1, source_target_pairs={{0,2},{1,3},{2,0},{3,1},{4,6},{5,7},{6,4},{7,5},{8,10},{9,11},{10,... | collective-permute-start | bytes 12582920 | tf_op jit(solution)/shard_map/ppermute | solution.py:16
  310.5 182.1 %collective-permute-start.2 = (f32[2048,512]{1,0:T(8,128)}, f32[2048,512]{1,0:T(8,128)}, u32[]{:S(2)}, u32[]{:S(2)}) collective-permute-start(f32[2048,512]{1,0:T(8,128)} %add.63), channel_id=1, source_target_pairs={{0,4},{1,5},{2,6},{3,7},{4,0},{5,1},{6,2},{7,3},{8,12},{9,13},{10,... | collective-permute-start | bytes 12582920 | tf_op jit(solution)/shard_map/ppermute | solution.py:16
  517.4 233.7 %all-reduce.6.cloned.1.call-start = ((), (), s32[]{:S(2)}) async-start(), calls=%async_computation.3 | async-start | bytes 2097152 | tf_op jit(solution)/shard_map/psum | solution.py:31
  688.4 4.3 copy-start
  698.5 6.9 copy-start.1
  705.4 1.0 copy-start.3
  714.2 366.2 %reduce-scatter.2.cloned.1.call-start = ((), (), s32[]{:S(2)}) async-start(), calls=%async_computation.4 | async-start | bytes 9175040 | tf_op jit(solution)/shard_map/reduce_scatter | solution.py:48
  754.1 1.0 copy-start.5
  898.1 4.7 copy-start.4
  906.9 1.0 copy-start.2
  1015.2 119.9 %all-gather.5.cloned.1.call-start = ((), (), s32[]{:S(2)}) async-start(), calls=%async_computation.5 | async-start | bytes 9175040 | tf_op jit(solution)/shard_map/all_gather | solution.py:51
Sparse Core Ops, SparseCore 0:
  9.5 56.0 all-gather.2
  517.5 36.2 all-reduce.3
  714.3 36.7 all-reduce.5
  1015.3 65.0 reduce-scatter.1
  1081.8 53.2 all-gather.4
